TPU v7x, 32 devices: a whole 2x2x4 slice. The times are simulated.
32 devices in a mesh: groups: 2 (over y), seq: 4 (over z), tp: 2 (over x), kv: 2 (over core).
Axes of the slice: x: 2, y: 2, z: 4, core: 2. Of those that a mesh axis runs over, the one named last changes fastest.
Arguments:
- events: bfloat16 [8, 512, 2048], P('groups', 'seq', ('tp', 'kv')), parts along dimension 0, may hold values from -6 to 6
- history_cache: bfloat16 [2, 8, 512, 1024], P(None, ('groups', 'seq'), None, ('tp', 'kv')), parts along dimension 1, may hold values from -6 to 6
- block_counts: int32 [8], P(('groups', 'seq')), parts along dimension 0, may hold values from 1 to 4
- semantic_ids: int32 [4, 128], P(None, ('groups', 'seq')), parts along dimension 1, may hold values from 0 to 4095
- beam_parents: int32 [3, 128], P(None, ('groups', 'seq')), parts along dimension 1, may hold values from 0 to 15
- query_weight: bfloat16 [2048, 2048], P('seq', ('tp', 'kv')), may hold values from -0.125 to 0.125
- keyval_weight: bfloat16 [2, 2048, 1024], P(None, 'seq', ('tp', 'kv')), may hold values from -0.125 to 0.125
- out_weight: bfloat16 [2048, 2048], P('seq', ('tp', 'kv')), may hold values from -0.125 to 0.125
- cross_weight: bfloat16 [2, 2048, 1024], P(None, 'seq', ('tp', 'kv')), may hold values from -0.125 to 0.125
- decoder_query: bfloat16 [2048, 2048], P(None, ('tp', 'kv')), may hold values from -0.125 to 0.125
- decoder_out: bfloat16 [2048, 2048], P(None, ('tp', 'kv')), may hold values from -0.125 to 0.125
- code_table: bfloat16 [4096, 2048], P(('tp', 'kv')), may hold values from -6 to 6
- encoder_gain: float32 [2048], replicated, may hold values from 0.25 to 1.75
- cross_gain: float32 [2048], replicated, may hold values from 0.25 to 1.75
- decoder_gain: float32 [2048], replicated, may hold values from 0.25 to 1.75
Outputs:
- encoded: bfloat16 [8, 512, 2048], P(('groups', 'seq'), ('tp', 'kv')), parts along dimension 0
- beam_state: bfloat16 [128, 2048], P(('groups', 'seq'), ('tp', 'kv')), parts along dimension 0
There are 2 independent parts, one for each index of `groups`. A program takes and returns all parts, laid end to end along the dimension named above; an argument that names none is the same for every part. Nothing has to cross between parts.
Inputs may be any that keep to these rules, and one draw needn't show every extreme that they name: A user's first 128 * block_counts new events are real; the rest are padding. `semantic_ids`: the codebook entry decoded for each beam row. `beam_parents`: the beam of the previous step that each beam row continues, counted among its user's 16 beams.
All inputs are finite; a program needn't handle non-finite values.
Results may differ from a plain program's by a relative error of at most 0.014.
Values may be sent and summed in bfloat16 or wider, within the bound.
A program may use at most 64 MiB of HBM per device.

v0:
```python
import jax
import jax.numpy as jnp
from jax import lax
from jax.sharding import PartitionSpec as P

H = 16
DH = 128
KVH = 8
BLK = 128
STEPS = 4
eps = 1e-06


def root_norm(values, scale_gain):
    mean_square = jnp.mean(values * values, axis=-1, keepdims=True)
    return values * lax.rsqrt(mean_square + eps) * scale_gain


def shards(
    events,
    history_cache,
    block_counts,
    semantic_ids,
    beam_parents,
    query_weight,
    keyval_weight,
    out_weight,
    cross_weight,
    decoder_query,
    decoder_out,
    code_table,
    encoder_gain,
    cross_gain,
    decoder_gain,
):
    head_size = DH
    group_ratio = H // KVH
    relayed = lax.all_to_all(events, "seq", split_axis=0, concat_axis=1, tiled=True)
    whole = lax.all_gather(relayed, ("tp", "kv"), axis=2, tiled=True)
    users = whole.shape[0]
    length = whole.shape[1]
    width = whole.shape[2]
    source = whole.reshape(users * length, width).astype(jnp.float32)
    normed = root_norm(source, encoder_gain).astype(jnp.bfloat16)
    query_cols = query_weight.shape[1]
    key_cols = keyval_weight.shape[2]
    joined = jnp.concatenate([query_weight, keyval_weight[0], keyval_weight[1]], axis=1)
    projected = jnp.dot(
        normed,
        lax.all_gather(joined, "seq", axis=0, tiled=True),
        preferred_element_type=jnp.float32,
    )
    queries = projected[:, :query_cols].astype(jnp.bfloat16)
    keys_new = projected[:, query_cols : query_cols + key_cols].astype(jnp.bfloat16)
    values_new = projected[:, query_cols + key_cols :].astype(jnp.bfloat16)
    out_full, cross_full = (
        lax.all_gather(out_weight, "seq", axis=0, tiled=True),
        lax.all_gather(cross_weight, "seq", axis=1, tiled=True),
    )
    key_groups = key_cols // head_size
    history_len = history_cache.shape[2]
    query_heads = queries.reshape(users, length, key_groups, group_ratio, head_size)
    key_heads = jnp.concatenate(
        [history_cache[0], keys_new.reshape(users, length, key_cols)], axis=1
    )
    key_heads = key_heads.reshape(users, history_len + length, key_groups, head_size)
    value_heads = jnp.concatenate(
        [history_cache[1], values_new.reshape(users, length, key_cols)], axis=1
    )
    value_heads = value_heads.reshape(users, history_len + length, key_groups, head_size)
    scores = jnp.einsum(
        "uigad,ujgd->ugaij", query_heads, key_heads, preferred_element_type=jnp.float32
    ) * head_size ** (-0.5)
    query_index = lax.broadcasted_iota(jnp.int32, (length, history_len + length), 0)
    key_index = lax.broadcasted_iota(jnp.int32, (length, history_len + length), 1) - history_len
    live_limit = (block_counts * BLK)[:, None, None, None, None]
    visible = (key_index < 0)[None, None, None] | (key_index <= query_index)[None, None, None] & (
        key_index[None, None, None] < live_limit
    )
    raised = jnp.where(visible, jnp.exp(scores), jnp.float32(0.0))
    denominator = jnp.sum(raised, axis=-1, keepdims=True)
    softened = (raised / denominator).astype(jnp.bfloat16)
    attended = jnp.einsum(
        "ugaij,ujgd->uigad", softened, value_heads, preferred_element_type=jnp.float32
    )
    attended = attended.astype(jnp.bfloat16).reshape(users * length, query_cols)
    group = lax.axis_index(("tp", "kv"))
    groups = lax.axis_size(("tp", "kv"))
    share = users * length // groups
    group_term = lax.dot_general(
        attended, out_full, (((1,), (1,)), ((), ())), preferred_element_type=jnp.float32
    ).astype(jnp.bfloat16)
    mixed = lax.psum(group_term, ("tp", "kv")).astype(jnp.float32)
    encoded_all = source + mixed
    cross_all = root_norm(encoded_all, cross_gain).astype(jnp.bfloat16)
    encoded_rows = lax.dynamic_slice_in_dim(encoded_all, group * share, share, 0)
    encoded_out = encoded_rows.astype(jnp.bfloat16).reshape(users, share // users, width)
    cross_keys = jnp.dot(cross_all, cross_full[0], preferred_element_type=jnp.float32).astype(
        jnp.bfloat16
    )
    cross_values = jnp.dot(cross_all, cross_full[1], preferred_element_type=jnp.float32).astype(
        jnp.bfloat16
    )
    cross_key_heads = cross_keys.reshape(users, length, key_groups, head_size)
    cross_value_heads = cross_values.reshape(users, length, key_groups, head_size)
    live_events = (
        lax.broadcasted_iota(jnp.int32, (users, length), 1) < (block_counts * BLK)[:, None]
    )
    live_mask = live_events[:, None, None, None, :]
    beam_rows = semantic_ids.shape[1]
    per_user = beam_rows // users
    vocab_rows = code_table.shape[0]
    vocab_ids = group * vocab_rows + lax.broadcasted_iota(jnp.int32, (1, vocab_rows), 1)

    def lookup(id_values):
        onehot = (id_values[:, None] == vocab_ids).astype(jnp.bfloat16)
        return jnp.dot(onehot, code_table, preferred_element_type=jnp.float32)

    def attend(beam_hidden):
        normed_beams = root_norm(beam_hidden, decoder_gain).astype(jnp.bfloat16)
        beam_queries = jnp.dot(
            normed_beams, decoder_query, preferred_element_type=jnp.float32
        ).astype(jnp.bfloat16)
        beam_queries = beam_queries.reshape(users, per_user, key_groups, group_ratio, head_size)
        beam_scores = jnp.einsum(
            "ubgad,ujgd->ugabj", beam_queries, cross_key_heads, preferred_element_type=jnp.float32
        ) * head_size ** (-0.5)
        beam_raised = jnp.where(live_mask, jnp.exp(beam_scores), jnp.float32(0.0))
        beam_total = jnp.sum(beam_raised, axis=-1, keepdims=True)
        beam_soft = (beam_raised / beam_total).astype(jnp.bfloat16)
        beam_attended = jnp.einsum(
            "ugabj,ujgd->ubgad", beam_soft, cross_value_heads, preferred_element_type=jnp.float32
        )
        beam_attended = beam_attended.astype(jnp.bfloat16).reshape(beam_rows, query_cols)
        return lax.dot_general(
            beam_attended, decoder_out, (((1,), (1,)), ((), ())), preferred_element_type=jnp.float32
        )

    def combine(beam_terms):
        return lax.psum(beam_terms.astype(jnp.bfloat16), ("tp", "kv")).astype(jnp.float32)

    local_rows = lax.broadcasted_iota(jnp.int32, (beam_rows,), 0)
    beam_hidden = combine(lookup(semantic_ids[0]))
    mixed_state = attend(beam_hidden)
    for level in range(1, STEPS):
        source_rows = local_rows // per_user * per_user + beam_parents[level - 1]
        moved = jnp.take(mixed_state, source_rows, axis=0) + lookup(semantic_ids[level])
        beam_hidden = jnp.take(beam_hidden, source_rows, axis=0) + combine(moved)
        mixed_state = attend(beam_hidden)
    finished = (beam_hidden + combine(mixed_state)).astype(jnp.bfloat16)
    width_share = width // groups
    beam_out = lax.dynamic_slice_in_dim(finished, group * width_share, width_share, 1)
    return (encoded_out, beam_out)


def solution(mesh):
    in_specs = (
        P("groups", "seq", ("tp", "kv")),
        P(None, ("groups", "seq"), None, ("tp", "kv")),
        P(("groups", "seq")),
        P(None, ("groups", "seq")),
        P(None, ("groups", "seq")),
        P("seq", ("tp", "kv")),
        P(None, "seq", ("tp", "kv")),
        P("seq", ("tp", "kv")),
        P(None, "seq", ("tp", "kv")),
        P(None, ("tp", "kv")),
        P(None, ("tp", "kv")),
        P(("tp", "kv"), None),
        P(),
        P(),
        P(),
    )
    out_specs = (P(("groups", "seq"), ("tp", "kv"), None), P(("groups", "seq"), ("tp", "kv")))
    return jax.shard_map(shards, mesh=mesh, in_specs=in_specs, out_specs=out_specs, check_vma=False)
```

profile of v0, /device:TPU:0, one launch (start us, length us, event | category | flops | bytes accessed | tf_op | source)
XLA Modules:
  0.0 447.2 jit_solution(481606835040528028)
XLA Ops:
  7.2 21.1 %all_to_all.12 = bf16[4,128,512]{2,1,0:T(8,128)(2,1)} all-to-all(bf16[4,128,512]{2,1,0:T(8,128)(2,1)} %param.17), channel_id=1, replica_groups=mesh['groups'=2,'seq'=4,'tp'=2,'kv'=2] {'seq'}, dimensions={0} | all-to-all | bytes 1048576 | tf_op jit(solution)/shard_map/all_to_all | solution.py:38
  28.4 1.1 slice_bitcast_fusion.5
  29.5 1.2 pad_maximum_fusion
  30.8 0.7 all-gather.9.cloned.1.call-update
  32.4 0.9 copy.37
  33.3 0.8 copy.34
  34.1 1.6 fusion.15
  35.7 3.5 convolution_convert_fusion.2
  39.2 11.0 %all-gather.5.cloned.1.call-done = bf16[1,512,2048]{2,1,0:T(8,128)(2,1)} async-done(((bf16[1,512,512]{2,1,0:T(8,128)(2,1)}), bf16[1,512,2048]{2,1,0:T(8,128)(2,1)}) %all-gather.5.cloned.1.call-update) | async-done | bytes 2097168 | tf_op jit(solution)/shard_map/all_gather | solution.py:39
  50.2 2.1 fusion.1
  52.3 80.3 %all-gather.7.cloned.1.call-done = bf16[2048,1024]{1,0:T(8,128)(2,1)} async-done(((bf16[512,1024]{1,0:T(8,128)(2,1)}), bf16[2048,1024]{1,0:T(8,128)(2,1)}) %all-gather.7.cloned.1.call-update) | async-done | bytes 4194320 | tf_op jit(solution)/shard_map/all_gather | solution.py:50
  132.5 5.2 %fusion.16 = bf16[512,1024]{1,0:T(8,128)(2,1)S(1)} fusion(bf16[2048,1024]{1,0:T(8,128)(2,1)} %all-gather.7.cloned.1.call-done, bf16[1,512,2048]{2,1,0:T(8,128)(2,1)} %all-gather.5.cloned.1.call-done, f32[2048]{0:T(1024)S(1)} %copy-done.13, f32[512]{0:T(512)S(1)} %add_rsqrt_fusion.1), kind=kOutput, calls=%fused_computation.35 | convolution fusion | flops 2152202240 | bytes 7350272 | tf_op jit(solution)/shard_map/dot_general | solution.py:48
  137.9 0.8 copy.38
  138.7 0.9 reshape.294
  139.8 3.6 fusion
  143.4 2.4 fusion.19
  145.8 32.5 %all-gather.9.cloned.1.call-done = bf16[2048,512]{1,0:T(8,128)(2,1)} async-done(((bf16[512,512]{1,0:T(8,128)(2,1)}), bf16[2048,512]{1,0:T(8,128)(2,1)}) %all-gather.9.cloned.1.call-update) | async-done | bytes 2097168 | tf_op jit(solution)/shard_map/all_gather | solution.py:57
  178.3 4.2 convolution_convert_fusion
  183.4 50.6 %all-reduce.15.cloned.1.call-done = (bf16[512,2048]{1,0:T(8,128)(2,1)}, bf16[16,2048]{1,0:T(8,128)(2,1)}) async-done(((bf16[512,2048]{1,0:T(8,128)(2,1)}, bf16[16,2048]{1,0:T(8,128)(2,1)}), (bf16[512,2048]{1,0:T(8,128)(2,1)}, bf16[16,2048]{1,0:T(8,128)(2,1)})) %all-reduce.15.cloned.1.call-update) | async-done | bytes 2162704 | tf_op jit(solution)/shard_map/psum | solution.py:93
  234.0 1.0 multiply_reduce_fusion.4
  235.0 2.1 convolution_convert_fusion.12
  237.0 3.0 multiply_reduce_fusion
  240.0 41.1 %all-gather.11.cloned.1.call-done = bf16[2,2048,256]{2,1,0:T(8,128)(2,1)} async-done(((bf16[2,512,256]{2,1,0:T(8,128)(2,1)}), bf16[2,2048,256]{2,1,0:T(8,128)(2,1)}) %all-gather.11.cloned.1.call-update) | async-done | bytes 2097168 | tf_op jit(solution)/shard_map/all_gather | solution.py:58
  281.2 3.8 convolution_convert_fusion.3
  285.6 1.2 convolution_convert_fusion.4
  287.1 0.6 fusion.92
  287.7 0.6 gather_fusion.1
  288.3 3.5 fusion.6
  292.6 29.8 %all-reduce.7.cloned.1.call-done = bf16[16,2048]{1,0:T(8,128)(2,1)} async-done(((bf16[16,2048]{1,0:T(8,128)(2,1)}), bf16[16,2048]{1,0:T(8,128)(2,1)}) %all-reduce.7.cloned.1.call-update) | async-done | bytes 65552 | tf_op jit(solution)/shard_map/psum | solution.py:140
  322.4 1.0 multiply_reduce_fusion.3
  323.5 2.0 convolution_convert_fusion.10
  326.0 0.6 fusion.93
  326.7 0.6 gather_fusion.3
  327.3 3.5 fusion.7
  331.5 31.0 %all-reduce.9.cloned.1.call-done = bf16[16,2048]{1,0:T(8,128)(2,1)} async-done(((bf16[16,2048]{1,0:T(8,128)(2,1)}), bf16[16,2048]{1,0:T(8,128)(2,1)}) %all-reduce.9.cloned.1.call-update) | async-done | bytes 65552 | tf_op jit(solution)/shard_map/psum | solution.py:140
  362.5 1.0 multiply_reduce_fusion.2
  363.6 2.0 convolution_convert_fusion.8
  366.2 0.6 fusion.94
  366.8 0.6 gather_fusion.5
  367.4 3.5 fusion.8
  371.0 4.4 convert_add_fusion
  376.1 26.6 %all-reduce.11.cloned.1.call-done = bf16[16,2048]{1,0:T(8,128)(2,1)} async-done(((bf16[16,2048]{1,0:T(8,128)(2,1)}), bf16[16,2048]{1,0:T(8,128)(2,1)}) %all-reduce.11.cloned.1.call-update) | async-done | bytes 65552 | tf_op jit(solution)/shard_map/psum | solution.py:140
  402.7 1.0 multiply_reduce_fusion.1
  403.7 2.0 convolution_convert_fusion.6
  406.3 1.3 convolution_convert_fusion.1
  407.6 1.9 fusion.42
  409.5 29.8 %all-reduce.13.cloned.1.call-done = bf16[16,2048]{1,0:T(8,128)(2,1)} async-done(((bf16[16,2048]{1,0:T(8,128)(2,1)}), bf16[16,2048]{1,0:T(8,128)(2,1)}) %all-reduce.13.cloned.1.call-update) | async-done | bytes 65552 | tf_op jit(solution)/shard_map/psum | solution.py:140
  439.3 1.3 fusion.66
  (92 shorter events, 6.2 us)
Async XLA Ops:
  7.2 279.9 %copy-start = (bf16[2048,512]{1,0:T(8,128)(2,1)S(1)}, bf16[2048,512]{1,0:T(8,128)(2,1)}, u32[]{:S(2)}) copy-start(bf16[2048,512]{1,0:T(8,128)(2,1)} %param.27) | copy-start | bytes 6291460
  7.2 22.3 %copy-start.6 = (bf16[512,512]{1,0:T(8,128)(2,1)S(1)}, bf16[512,512]{1,0:T(8,128)(2,1)}, u32[]{:S(2)}) copy-start(bf16[512,512]{1,0:T(8,128)(2,1)} %param.22) | copy-start | bytes 1572868
  7.2 43.0 %all-gather.5.cloned.1.call-start = ((), (), s32[]{:S(2)}) async-start(), calls=%async_computation.1 | async-start | bytes 2621440 | tf_op jit(solution)/shard_map/all_gather | solution.py:39
  28.3 104.2 %all-gather.7.cloned.1.call-start = ((), (), s32[]{:S(2)}) async-start(), calls=%async_computation.2 | async-start | bytes 5242880 | tf_op jit(solution)/shard_map/all_gather | solution.py:50
  29.5 2.7 copy-start.4
  30.7 3.4 copy-start.10
  30.7 147.6 %all-gather.9.cloned.1.call-start = ((), (), s32[]{:S(2)}) async-start(), calls=%async_computation.3 | async-start | bytes 2621440 | tf_op jit(solution)/shard_map/all_gather | solution.py:57
  31.5 202.5 %all-reduce.15.cloned.1.call-start = ((), (), s32[]{:S(2)}) async-start(), calls=%async_computation.9 | async-start | bytes 4325376 | tf_op jit(solution)/shard_map/psum | solution.py:93
  39.2 93.3 %copy-start.13 = (f32[2048]{0:T(1024)S(1)}, f32[2048]{0:T(1024)}, u32[]{:S(2)}) copy-start(f32[2048]{0:T(1024)} %param.29) | copy-start | bytes 24580
  137.9 1.9 copy-start.8
  139.8 3.6 copy-start.5
  139.8 3.6 copy-start.7
  182.5 0.9 copy-start.11
  182.5 52.4 %copy-start.9 = (f32[2048]{0:T(1024)S(1)}, f32[2048]{0:T(1024)}, u32[]{:S(2)}) copy-start(f32[2048]{0:T(1024)} %param.31) | copy-start | bytes 24580
  182.5 98.6 %all-gather.11.cloned.1.call-start = ((), (), s32[]{:S(2)}) async-start(), calls=%async_computation.4 | async-start | bytes 2621440 | tf_op jit(solution)/shard_map/all_gather | solution.py:58
  183.1 139.3 %all-reduce.7.cloned.1.call-start = ((), (), s32[]{:S(2)}) async-start(), calls=%async_computation.5 | async-start | bytes 131072 | tf_op jit(solution)/shard_map/psum | solution.py:140
  237.0 44.1 %copy-start.14 = (f32[2048]{0:T(1024)S(1)}, f32[2048]{0:T(1024)}, u32[]{:S(2)}) copy-start(f32[2048]{0:T(1024)} %param.30) | copy-start | bytes 24580
  281.2 4.0 copy-start.1
  281.2 4.0 copy-start.2
  281.2 4.4 copy-start.12
  288.3 3.6 copy-start.3
  291.9 70.6 %all-reduce.9.cloned.1.call-start = ((), (), s32[]{:S(2)}) async-start(), calls=%async_computation.6 | async-start | bytes 131072 | tf_op jit(solution)/shard_map/psum | solution.py:140
  330.8 71.8 %all-reduce.11.cloned.1.call-start = ((), (), s32[]{:S(2)}) async-start(), calls=%async_computation.7 | async-start | bytes 131072 | tf_op jit(solution)/shard_map/psum | solution.py:140
  371.0 68.3 %all-reduce.13.cloned.1.call-start = ((), (), s32[]{:S(2)}) async-start(), calls=%async_computation.8 | async-start | bytes 131072 | tf_op jit(solution)/shard_map/psum | solution.py:140
Sparse Core Ops, SparseCore 0:
  28.5 21.6 all-gather.4
  51.8 80.7 all-gather.6
  134.1 44.1 all-gather.8
  182.7 51.2 all-reduce.14
  235.4 45.7 all-gather.10
  292.0 30.3 all-reduce.6
  331.0 31.5 all-reduce.8
  371.1 31.5 all-reduce.10
  407.7 31.5 all-reduce.12
where the time goes:
time: 448 us; the launch traced here: 447 us
  waiting for transfers between devices  334 us (75%)
  matrix products  47.6 us (11%)
  blocking collectives  21.1 us (5%)
  other arithmetic  17.9 us (4%)
  between operations  14.9 us (3%)
  local copies, waits for them, and re-layouts  11.2 us (2%)
    psum x4, waiting for transfers between devices, combine(): lax.psum(beam_terms.astype(jnp.bfloat16), ('tp', 'kv')).astype(jnp.float32)  117 us
    all_gather x1, waiting for transfers between devices, shards(): lax.all_gather(joined, 'seq', axis=0, tiled=True)  80.3 us
    psum x1, waiting for transfers between devices, shards(): mixed = lax.psum(group_term, ('tp', 'kv')).astype(jnp.float32)  50.6 us
    all_gather x1, waiting for transfers between devices, shards(): lax.all_gather(cross_weight, 'seq', axis=1, tiled=True)  41.1 us
    all_gather x1, waiting for transfers between devices, shards(): lax.all_gather(out_weight, 'seq', axis=0, tiled=True)  32.5 us
    all_to_all x1, blocking collectives, shards(): lax.all_to_all(events, 'seq', split_axis=0, concat_axis=1, tiled=True)  21.1 us
    dot_general x4, matrix products, lookup(): return jnp.dot(onehot, code_table, preferred_element_type=jnp.float32)  14.1 us
    all_gather x1, waiting for transfers between devices, shards(): whole = lax.all_gather(relayed, ('tp', 'kv'), axis=2, tiled=True)  11 us
  transfers between devices with their start and end apart: 9, of which 9 were waited for; matrix products, arithmetic and copies ran while one was open for 9% of the time, Pallas kernels for 0%

commit v1 on v0

--- a/solution.py
+++ b/solution.py
@@ -9,6 +9,12 @@
 BLK = 128
 STEPS = 4
 eps = 1e-06
+
+
+def add_all(block, mesh_axis):
+    parts = lax.all_gather(block, mesh_axis, axis=0, tiled=False)
+    total = parts.sum(axis=0)
+    return total
 
 
 def root_norm(values, scale_gain):
@@ -137,7 +143,7 @@
         )
 
     def combine(beam_terms):
-        return lax.psum(beam_terms.astype(jnp.bfloat16), ("tp", "kv")).astype(jnp.float32)
+        return add_all(beam_terms.astype(jnp.bfloat16), ("tp", "kv")).astype(jnp.float32)
 
     local_rows = lax.broadcasted_iota(jnp.int32, (beam_rows,), 0)
     beam_hidden = combine(lookup(semantic_ids[0]))

time: 448 us -> 345 us (0.77)
  waiting for transfers between devices: 334 us -> 210 us
  blocking collectives: 21.1 us -> 52.3 us
  other arithmetic: 17.9 us -> 12.5 us
    psum x4 -> x0, waiting for transfers between devices: 117 us -> none  [combine(): lax.psum(beam_terms.astype(jnp.bfloat16), ('tp', 'kv')).astype(jnp.float32)]
    all_gather x0 -> x5, blocking collectives: none -> 31.2 us  [add_all(): parts = lax.all_gather(block, mesh_axis, axis=0, tiled=False)]
    psum x1, waiting for transfers between devices: 50.6 us -> 36.8 us  [shards(): mixed = lax.psum(group_term, ('tp', 'kv')).astype(jnp.float32)]
  transfers between devices with their start and end apart: 9 -> 5, of which waited for: 9 -> 5; matrix products, arithmetic and copies ran while one was open for 9% -> 9% of each run, Pallas kernels for 0% -> 0%
where the time goes in v1:
time: 345 us; the launch traced here: 344 us
  waiting for transfers between devices  210 us (61%)
  blocking collectives  52.3 us (15%)
  matrix products  44.4 us (13%)
  between operations  14.9 us (4%)
  other arithmetic  12.5 us (4%)
  local copies, waits for them, and re-layouts  10.2 us (3%)
    all_gather x1, waiting for transfers between devices, shards(): lax.all_gather(joined, 'seq', axis=0, tiled=True)  80.3 us
    all_gather x1, waiting for transfers between devices, shards(): lax.all_gather(cross_weight, 'seq', axis=1, tiled=True)  44.2 us
    psum x1, waiting for transfers between devices, shards(): mixed = lax.psum(group_term, ('tp', 'kv')).astype(jnp.float32)  36.8 us
    all_gather x1, waiting for transfers between devices, shards(): lax.all_gather(out_weight, 'seq', axis=0, tiled=True)  32.6 us
    all_gather x5, blocking collectives, add_all(): parts = lax.all_gather(block, mesh_axis, axis=0, tiled=False)  31.2 us
    all_to_all x1, blocking collectives, shards(): lax.all_to_all(events, 'seq', split_axis=0, concat_axis=1, tiled=True)  21.1 us
    all_gather x1, waiting for transfers between devices, shards(): whole = lax.all_gather(relayed, ('tp', 'kv'), axis=2, tiled=True)  14.5 us
    dot_general x4, matrix products, lookup(): return jnp.dot(onehot, code_table, preferred_element_type=jnp.float32)  11.6 us
  transfers between devices with their start and end apart: 5, of which 5 were waited for; matrix products, arithmetic and copies ran while one was open for 9% of the time, Pallas kernels for 0%

profile of v1, /device:TPU:0, one launch (start us, length us, event | category | flops | bytes accessed | tf_op | source)
XLA Modules:
  0.0 344.0 jit_solution(4878761425732444620)
XLA Ops:
  7.2 21.1 %all_to_all.12 = bf16[4,128,512]{2,1,0:T(8,128)(2,1)} all-to-all(bf16[4,128,512]{2,1,0:T(8,128)(2,1)} %param.17), channel_id=1, replica_groups=mesh['groups'=2,'seq'=4,'tp'=2,'kv'=2] {'seq'}, dimensions={0} | all-to-all | bytes 1048576 | tf_op jit(solution)/shard_map/all_to_all | solution.py:44
  28.4 1.1 slice_bitcast_fusion.5
  29.5 1.2 pad_maximum_fusion
  30.8 0.7 all-gather.14.cloned.1.call-update
  32.4 0.9 copy.37
  33.3 0.9 copy.34
  34.1 1.6 fusion.15
  35.7 14.5 %all-gather.10.cloned.1.call-done = bf16[1,512,2048]{2,1,0:T(8,128)(2,1)} async-done(((bf16[1,512,512]{2,1,0:T(8,128)(2,1)}), bf16[1,512,2048]{2,1,0:T(8,128)(2,1)}) %all-gather.10.cloned.1.call-update) | async-done | bytes 2097168 | tf_op jit(solution)/shard_map/all_gather | solution.py:45
  50.2 2.1 fusion.1
  52.3 80.3 %all-gather.12.cloned.1.call-done = bf16[2048,1024]{1,0:T(8,128)(2,1)} async-done(((bf16[512,1024]{1,0:T(8,128)(2,1)}), bf16[2048,1024]{1,0:T(8,128)(2,1)}) %all-gather.12.cloned.1.call-update) | async-done | bytes 4194320 | tf_op jit(solution)/shard_map/all_gather | solution.py:56
  132.5 5.2 %fusion.16 = bf16[512,1024]{1,0:T(8,128)(2,1)S(1)} fusion(bf16[2048,1024]{1,0:T(8,128)(2,1)} %all-gather.12.cloned.1.call-done, bf16[1,512,2048]{2,1,0:T(8,128)(2,1)} %all-gather.10.cloned.1.call-done, f32[2048]{0:T(1024)S(1)} %copy-done.12, f32[512]{0:T(512)S(1)} %add_rsqrt_fusion.1), kind=kOutput, calls=%fused_computation.35 | convolution fusion | flops 2152202240 | bytes 7350272 | tf_op jit(solution)/shard_map/dot_general | solution.py:54
  137.9 0.7 copy.38
  138.7 0.9 reshape.294
  139.7 3.6 %fusion = (f32[2,2,512]{2,1,0:T(2,128)S(1)}, f32[2,1024,512,2]{2,1,3,0:T(8,128)S(1)}) fusion(pred[512,1024]{0,1:T(8,128)(4,1)} %fusion.15, bf16[512,2,2,128]{3,2,1,0:T(2,128)(2,1)} %reshape.294, bf16[1,512,2,128]{3,1,2,0:T(8,128)(2,1)} %copy.38, bf16[1,512,2,128]{3,1,2,0:T(8,128)(2,1)S(1)} %copy-done.7), kind=kOutput, calls=%fused_computation.8 | convolution fusion | flops 544208896 | bytes 9969664 | tf_op jit(solution)/shard_map/uigad,ujgd->ugaij/dot_general | solution.py:77
  143.3 2.4 fusion.19
  145.7 32.6 %all-gather.14.cloned.1.call-done = bf16[2048,512]{1,0:T(8,128)(2,1)} async-done(((bf16[512,512]{1,0:T(8,128)(2,1)}), bf16[2048,512]{1,0:T(8,128)(2,1)}) %all-gather.14.cloned.1.call-update) | async-done | bytes 2097168 | tf_op jit(solution)/shard_map/all_gather | solution.py:63
  178.3 4.2 %convolution_convert_fusion = bf16[512,2048]{1,0:T(8,128)(2,1)} fusion(bf16[512,512]{0,1:T(8,128)(2,1)S(1)} %bitcast.216, bf16[2048,512]{1,0:T(8,128)(2,1)} %all-gather.14.cloned.1.call-done), kind=kOutput, calls=%fused_computation.19 | convolution fusion | flops 1074790400 | bytes 4718592 | tf_op jit(solution)/shard_map/dot_general | solution.py:96
  183.2 2.9 convolution_convert_fusion.2
  186.1 7.9 %all-gather = bf16[64,2048]{1,0:T(8,128)(2,1)S(1)} all-gather(bf16[16,2048]{1,0:T(8,128)(2,1)S(1)} %convolution_convert_fusion.2), channel_id=2, replica_groups=mesh['groups'=2,'seq'=4,'tp'=2,'kv'=2] {'tp','kv'}, dimensions={0}, use_global_device_ids=true | all-gather | bytes 327680 | tf_op jit(solution)/shard_map/all_gather | solution.py:15
  194.2 2.0 convolution_convert_fusion.12
  196.3 0.6 gather_fusion
  196.9 36.8 %all-reduce.2.cloned.1.call-done = bf16[512,2048]{1,0:T(8,128)(2,1)} async-done(((bf16[512,2048]{1,0:T(8,128)(2,1)}), bf16[512,2048]{1,0:T(8,128)(2,1)}) %all-reduce.2.cloned.1.call-update) | async-done | bytes 2097168 | tf_op jit(solution)/shard_map/psum | solution.py:99
  233.8 3.0 multiply_reduce_fusion
  236.7 44.2 %all-gather.16.cloned.1.call-done = bf16[2,2048,256]{2,1,0:T(8,128)(2,1)} async-done(((bf16[2,512,256]{2,1,0:T(8,128)(2,1)}), bf16[2,2048,256]{2,1,0:T(8,128)(2,1)}) %all-gather.16.cloned.1.call-update) | async-done | bytes 2097168 | tf_op jit(solution)/shard_map/all_gather | solution.py:64
  281.0 3.8 %convolution_convert_fusion.3 = bf16[512,256]{0,1:T(8,128)(2,1)S(1)} fusion(bf16[2,2048,256]{2,1,0:T(8,128)(2,1)} %all-gather.16.cloned.1.call-done, f32[2048]{0:T(1024)S(1)} %copy-done.13, f32[512]{0:T(512)S(1)} %add_rsqrt_fusion, bf16[512,2048]{1,0:T(8,128)(2,1)} %all-reduce.2.cloned.1.call-done, bf16[1,512,2048]{2,1,0:T(8,128)(2,1)} %all-gather.10.cloned.1.call-done), kind=kOutput, calls=%fused_computation.37 | convolution fusion | flops 543293440 | bytes 5515264 | tf_op jit(solution)/shard_map/dot_general | solution.py:104
  285.4 1.2 convolution_convert_fusion.4
  286.8 0.6 fusion.92
  287.5 0.6 gather_fusion.1
  288.1 2.9 fusion.6
  291.0 5.8 %all-gather.1 = bf16[64,2048]{1,0:T(8,128)(2,1)S(1)} all-gather(bf16[16,2048]{1,0:T(8,128)(2,1)S(1)} %fusion.6), channel_id=3, replica_groups=mesh['groups'=2,'seq'=4,'tp'=2,'kv'=2] {'tp','kv'}, dimensions={0}, use_global_device_ids=true | all-gather | bytes 327680 | tf_op jit(solution)/shard_map/all_gather | solution.py:15
  297.0 2.0 convolution_convert_fusion.10
  299.6 0.6 fusion.93
  300.2 0.6 gather_fusion.2
  300.9 0.6 gather_fusion.3
  301.5 2.9 fusion.7
  304.4 5.8 %all-gather.2 = bf16[64,2048]{1,0:T(8,128)(2,1)S(1)} all-gather(bf16[16,2048]{1,0:T(8,128)(2,1)S(1)} %fusion.7), channel_id=4, replica_groups=mesh['groups'=2,'seq'=4,'tp'=2,'kv'=2] {'tp','kv'}, dimensions={0}, use_global_device_ids=true | all-gather | bytes 327680 | tf_op jit(solution)/shard_map/all_gather | solution.py:15
  310.5 2.0 convolution_convert_fusion.8
  313.0 0.6 fusion.94
  313.7 0.6 gather_fusion.4
  314.3 0.6 gather_fusion.5
  314.9 2.9 fusion.8
  317.8 5.8 %all-gather.3 = bf16[64,2048]{1,0:T(8,128)(2,1)S(1)} all-gather(bf16[16,2048]{1,0:T(8,128)(2,1)S(1)} %fusion.8), channel_id=5, replica_groups=mesh['groups'=2,'seq'=4,'tp'=2,'kv'=2] {'tp','kv'}, dimensions={0}, use_global_device_ids=true | all-gather | bytes 327680 | tf_op jit(solution)/shard_map/all_gather | solution.py:15
  323.9 2.0 convolution_convert_fusion.6
  326.5 0.6 convolution_convert_fusion.1
  327.1 5.9 %all-gather.4 = bf16[64,2048]{1,0:T(8,128)(2,1)S(1)} all-gather(bf16[16,2048]{1,0:T(8,128)(2,1)S(1)} %convolution_convert_fusion.1), channel_id=6, replica_groups=mesh['groups'=2,'seq'=4,'tp'=2,'kv'=2] {'tp','kv'}, dimensions={0}, use_global_device_ids=true | all-gather | bytes 327680 | tf_op jit(solution)/shard_map/all_gather | solution.py:15
  333.0 0.6 fusion.66
  333.6 3.0 convert_add_fusion
  336.7 0.8 fusion.42
  (88 shorter events, 5.0 us)
Async XLA Ops:
  7.2 279.7 %copy-start = (bf16[2048,512]{1,0:T(8,128)(2,1)S(1)}, bf16[2048,512]{1,0:T(8,128)(2,1)}, u32[]{:S(2)}) copy-start(bf16[2048,512]{1,0:T(8,128)(2,1)} %param.27) | copy-start | bytes 6291460
  7.2 22.3 %copy-start.5 = (bf16[512,512]{1,0:T(8,128)(2,1)S(1)}, bf16[512,512]{1,0:T(8,128)(2,1)}, u32[]{:S(2)}) copy-start(bf16[512,512]{1,0:T(8,128)(2,1)} %param.22) | copy-start | bytes 1572868
  7.2 43.0 %all-gather.10.cloned.1.call-start = ((), (), s32[]{:S(2)}) async-start(), calls=%async_computation.1 | async-start | bytes 2621440 | tf_op jit(solution)/shard_map/all_gather | solution.py:45
  28.3 104.2 %all-gather.12.cloned.1.call-start = ((), (), s32[]{:S(2)}) async-start(), calls=%async_computation.2 | async-start | bytes 5242880 | tf_op jit(solution)/shard_map/all_gather | solution.py:56
  29.5 2.7 copy-start.3
  30.7 147.6 %all-gather.14.cloned.1.call-start = ((), (), s32[]{:S(2)}) async-start(), calls=%async_computation.3 | async-start | bytes 2621440 | tf_op jit(solution)/shard_map/all_gather | solution.py:63
  31.5 202.3 %all-reduce.2.cloned.1.call-start = ((), (), s32[]{:S(2)}) async-start(), calls=%async_computation.4 | async-start | bytes 4194304 | tf_op jit(solution)/shard_map/psum | solution.py:99
  32.2 100.3 %copy-start.12 = (f32[2048]{0:T(1024)S(1)}, f32[2048]{0:T(1024)}, u32[]{:S(2)}) copy-start(f32[2048]{0:T(1024)} %param.29) | copy-start | bytes 24580
  137.9 1.8 copy-start.7
  139.7 3.6 %copy-start.4 = (pred[512,1024]{0,1:T(8,128)(4,1)S(1)}, pred[512,1024]{0,1:T(8,128)(4,1)}, u32[]{:S(2)}) copy-start(pred[512,1024]{0,1:T(8,128)(4,1)} %fusion.15) | copy-start | bytes 1572868
  139.7 3.6 %copy-start.6 = (bf16[1,1,512,256]{2,3,1,0:T(8,128)(2,1)S(1)}, bf16[1,1,512,256]{2,3,1,0:T(8,128)(2,1)}, u32[]{:S(2)}) copy-start(bf16[1,1,512,256]{2,3,1,0:T(8,128)(2,1)} %copy.34) | copy-start | bytes 786436
  182.5 0.7 copy-start.9
  182.5 98.4 %all-gather.16.cloned.1.call-start = ((), (), s32[]{:S(2)}) async-start(), calls=%async_computation.5 | async-start | bytes 2621440 | tf_op jit(solution)/shard_map/all_gather | solution.py:64
  183.2 11.0 %copy-start.8 = (f32[2048]{0:T(1024)S(1)}, f32[2048]{0:T(1024)}, u32[]{:S(2)}) copy-start(f32[2048]{0:T(1024)} %param.31) | copy-start | bytes 24580
  186.1 10.2 %copy-start.10 = (s32[3,16]{1,0:T(4,128)S(1)}, s32[3,16]{1,0:T(4,128)}, u32[]{:S(2)}) copy-start(s32[3,16]{1,0:T(4,128)} %param.21) | copy-start | bytes 580
  196.9 84.0 %copy-start.13 = (f32[2048]{0:T(1024)S(1)}, f32[2048]{0:T(1024)}, u32[]{:S(2)}) copy-start(f32[2048]{0:T(1024)} %param.30) | copy-start | bytes 24580
  280.9 4.0 %copy-start.1 = (bf16[1,512,2048]{2,1,0:T(8,128)(2,1)S(1)}, bf16[1,512,2048]{2,1,0:T(8,128)(2,1)}, u32[]{:S(2)}) copy-start(bf16[1,512,2048]{2,1,0:T(8,128)(2,1)} %all-gather.10.cloned.1.call-done) | copy-start | bytes 6291460
  280.9 4.0 %copy-start.2 = (bf16[512,2048]{1,0:T(8,128)(2,1)S(1)}, bf16[512,2048]{1,0:T(8,128)(2,1)}, u32[]{:S(2)}) copy-start(bf16[512,2048]{1,0:T(8,128)(2,1)} %all-reduce.2.cloned.1.call-done) | copy-start | bytes 6291460
  280.9 4.4 %copy-start.11 = (bf16[2,2048,256]{2,1,0:T(8,128)(2,1)S(1)}, bf16[2,2048,256]{2,1,0:T(8,128)(2,1)}, u32[]{:S(2)}) copy-start(bf16[2,2048,256]{2,1,0:T(8,128)(2,1)} %all-gather.16.cloned.1.call-done) | copy-start | bytes 6291460
Sparse Core Ops, SparseCore 0:
  28.5 21.6 all-gather.9
  51.8 80.7 all-gather.11
  134.1 44.1 all-gather.13
  182.6 51.0 all-reduce.1
  235.2 45.7 all-gather.15
